TPU v7x, 128 devices: a whole 4x4x4 slice. The times are simulated.
128 devices in a mesh: section: 4 (over z), mp: 32 (over y, x, core).
Axes of the slice: x: 4, y: 4, z: 4, core: 2. Of those that a mesh axis runs over, the one named last changes fastest.
Arguments:
- entering_hidden: bfloat16 [4, 256, 8192], P('section', None, 'mp'), may hold values from -12 to 12
- section_weight: bfloat16 [4, 8192, 8192], P('section', None, 'mp'), may hold values from -0.0625 to 0.0625
- section_norm_gain: bfloat16 [4, 8192], P('section', 'mp'), may hold values from 0.5 to 1.5
- plugin_narrowing_factors: bfloat16 [4, 32, 8192, 64], P('section', 'mp'), may hold values from -0.0625 to 0.0625
- plugin_widening_factors: bfloat16 [4, 32, 64, 8192], P('section', 'mp'), may hold values from -0.75 to 0.75
- reward_head: bfloat16 [8192], P('mp'), may hold values from -0.0625 to 0.0625
- adapter_of_block: int32 [4, 2], replicated, may hold values from 0 to 31
- live_block_rows: int32 [4, 2], P('section'), may hold values from 1 to 128
Outputs:
- hidden_out: bfloat16 [4, 256, 8192], P('section', None, 'mp')
- scores: float32 [4, 256], P('section')
All inputs are finite; a program needn't handle non-finite values.
Results may differ from a plain program's by a relative error of at most 0.022.
Values may be sent and summed in bfloat16 or wider, within the bound.
A program may use at most 64 MiB of HBM per device.

v0:
```python
import jax
import jax.numpy as jnp
from jax import lax
from jax.sharding import PartitionSpec as P

BLOCK = 128


def shifted(value, axis, steps):
    count = lax.axis_size(axis)
    initial, last = (max(0, -steps), min(count, count - steps))
    return lax.ppermute(value, axis, [(source, source + steps) for source in range(initial, last)])


def shards(
    entering_hidden,
    section_weight,
    section_norm_gain,
    plugin_narrowing_factors,
    plugin_widening_factors,
    reward_head,
    adapter_of_block,
    live_block_rows,
):
    sections = lax.axis_size("section")
    section_index = lax.axis_index("section")
    owners = lax.axis_size("mp")
    owner_index = lax.axis_index("mp")
    batches_here, rows, piece_extent = entering_hidden.shape
    micro = batches_here * sections
    width = piece_extent * owners
    blocks = rows // BLOCK
    owned_blocks = plugin_narrowing_factors.shape[1]
    adapters = owned_blocks * owners
    rank_position = plugin_narrowing_factors.shape[3]
    weight = section_weight[0]
    gain = section_norm_gain[0].astype(jnp.float32)
    fed = lax.all_gather(entering_hidden, "section", axis=0, tiled=True)
    up_map_columns = lax.all_to_all(
        plugin_widening_factors, "mp", split_axis=3, concat_axis=1, tiled=True
    )[0]
    up_table = up_map_columns.reshape(adapters, rank_position * piece_extent)

    def layer_of_section(hidden_state, adapter_numbers):
        hidden_f = hidden_state.astype(jnp.float32)
        onehot = (
            adapter_numbers[:, None] == jnp.arange(adapters, dtype=jnp.int32)[None, :]
        ).astype(jnp.bfloat16)
        squares = lax.psum(jnp.sum(hidden_f * hidden_f, axis=1), "mp")
        rescaled_activation = (
            hidden_f * lax.rsqrt(squares / width + 1e-05)[:, None] * gain[None, :]
        ).astype(jnp.bfloat16)
        gathered = lax.all_gather(rescaled_activation, "mp", axis=1, tiled=True)
        base = jnp.dot(gathered, weight, preferred_element_type=jnp.float32)
        local_ids = adapter_numbers - owner_index * owned_blocks
        mine = (local_ids >= 0) & (local_ids < owned_blocks)
        products = []
        for block_number in range(blocks):
            segment = gathered[block_number * BLOCK : (block_number + 1) * BLOCK]
            picked = jnp.clip(local_ids[block_number], 0, owned_blocks - 1)
            products.append(
                lax.cond(
                    mine[block_number],
                    lambda incoming_rows, selected_adapter: jnp.dot(
                        incoming_rows,
                        plugin_narrowing_factors[0, selected_adapter],
                        preferred_element_type=jnp.float32,
                    ),
                    lambda incoming_rows, selected_adapter: jnp.zeros(
                        (BLOCK, rank_position), jnp.float32
                    ),
                    segment,
                    picked,
                )
            )
        compressed_projection = jnp.stack(products)
        compressed_projection = lax.psum(compressed_projection.astype(jnp.bfloat16), "mp")
        chosen_expansion_matrix = (
            jnp.dot(onehot, up_table, preferred_element_type=jnp.float32)
            .astype(jnp.bfloat16)
            .reshape(blocks, rank_position, piece_extent)
        )
        thin_correction = jnp.einsum(
            "sin,sny->siy",
            compressed_projection,
            chosen_expansion_matrix,
            preferred_element_type=jnp.float32,
        ).reshape(rows, piece_extent)
        return (hidden_f + base + 2.0 * thin_correction).astype(jnp.bfloat16)

    def tick(step, carry):
        moving, finished = carry
        arrived = shifted(moving, "section", 1)
        feed_now = lax.dynamic_index_in_dim(fed, jnp.minimum(step, micro - 1), 0, keepdims=False)
        current_signal = jnp.where(section_index == 0, feed_now, arrived)
        selected_adapter = step - section_index
        valid = (selected_adapter >= 0) & (selected_adapter < micro)
        position = jnp.clip(selected_adapter, 0, micro - 1)
        adapter_numbers = lax.dynamic_index_in_dim(adapter_of_block, position, 0, keepdims=False)
        output = layer_of_section(current_signal, adapter_numbers)
        entry_tuple = valid & (section_index == sections - 1)
        previous = lax.dynamic_index_in_dim(finished, position, 0, keepdims=False)
        finished = lax.dynamic_update_index_in_dim(
            finished, jnp.where(entry_tuple, output, previous), position, 0
        )
        return (output, finished)

    start_moving = jnp.zeros((rows, piece_extent), jnp.bfloat16)
    start_finished = jnp.zeros((micro, rows, piece_extent), jnp.bfloat16)
    moving, finished = lax.fori_loop(0, micro + sections - 1, tick, (start_moving, start_finished))
    hidden_out = lax.psum_scatter(
        finished.astype(jnp.float32).astype(jnp.bfloat16),
        "section",
        scatter_dimension=0,
        tiled=True,
    )
    partial_score = jnp.sum(
        hidden_out.astype(jnp.float32) * reward_head.astype(jnp.float32)[None, None, :], axis=2
    )
    raw = lax.psum(partial_score, "mp")
    place = jnp.arange(rows, dtype=jnp.int32) % BLOCK
    limits = jnp.repeat(live_block_rows, BLOCK, axis=1)
    scores = jnp.where(place[None, :] < limits, raw, jnp.float32(0.0))
    return (hidden_out, scores)


def solution(mesh):
    placed = (
        P("section", None, "mp"),
        P("section", None, "mp"),
        P("section", "mp"),
        P("section", "mp", None, None),
        P("section", "mp", None, None),
        P("mp"),
        P(),
        P("section", None),
    )
    return jax.shard_map(
        shards,
        mesh=mesh,
        in_specs=placed,
        out_specs=(P("section", None, "mp"), P("section", None)),
        check_vma=False,
    )
```

profile of v0, /device:TPU:0, one launch (start us, length us, event | category | flops | bytes accessed | tf_op | source)
XLA Modules:
  0.0 1954.4 jit_solution(13879705828689722286)
XLA Ops:
  17.7 45.2 %reduce.1 = bf16[8192,64]{1,0:T(8,128)(2,1)S(1)} reduce(bf16[8192,1,1,64]{3,2,1,0:T(2,128)(2,1)} %bitcast.80, bf16[]{:T(256)} %broadcast.105), dimensions={1,2}, to_apply=%bitcast.49.reduce_sub_computation | reduce | bytes 2097154
  106.2 1752.9 %while.17 = (s32[]{:T(128)}, bf16[256,256]{1,0:T(8,128)(2,1)}, bf16[4,256,256]{2,1,0:T(8,128)(2,1)}, pred[]{:T(512)}, bf16[4,256,256]{2,1,0:T(8,128)(2,1)}, /*in...) while((s32[]{:T(128)}, bf16[256,256]{1,0:T(8,128)(2,1)}, ...), condition=%wide.region_8.9_spmd.clone, body=%wide.region_0.8_spmd.clone.sunk | while | flops 1353712128 | bytes 31792572 | solution.py:110
  114.1 63.3 %psum.36 = f32[256]{0:T(256)S(1)} all-reduce(f32[256]{0:T(256)S(1)} %get-tuple-element.499), channel_id=1, replica_groups=mesh['section'=4,'mp'=32] {'mp'}, use_global_device_ids=true, to_apply=%region_2.2 | all-reduce | flops 256 | bytes 2048 | tf_op jit(solution)/shard_map/while/body/eval_jaxpr/psum | solution.py:49
  181.2 43.1 %all-gather.2.cloned.1.call-done = bf16[256,8192]{1,0:T(8,128)(2,1)} async-done(((bf16[256,256]{1,0:T(8,128)(2,1)}), bf16[256,8192]{1,0:T(8,128)(2,1)}) %all-gather.2.cloned.1.call-update) | async-done | bytes 4194320 | tf_op jit(solution)/shard_map/while/body/eval_jaxpr/all_gather | solution.py:53
  224.3 126.5 %psum.37 = bf16[2,128,64]{1,2,0:T(8,128)(2,1)S(1)} all-reduce(bf16[2,128,64]{1,2,0:T(8,128)(2,1)S(1)} %pad_maximum_fusion.2), channel_id=1, replica_groups=mesh['section'=4,'mp'=32] {'mp'}, use_global_device_ids=true, to_apply=%region_7.7 | all-reduce | flops 16384 | bytes 65536 | tf_op jit(solution)/shard_map/while/body/eval_jaxpr/psum | solution.py:77
  364.4 62.7 %psum.36 = f32[256]{0:T(256)S(1)} all-reduce(f32[256]{0:T(256)S(1)} %get-tuple-element.499), channel_id=1, replica_groups=mesh['section'=4,'mp'=32] {'mp'}, use_global_device_ids=true, to_apply=%region_2.2 | all-reduce | flops 256 | bytes 2048 | tf_op jit(solution)/shard_map/while/body/eval_jaxpr/psum | solution.py:49
  430.9 42.9 %all-gather.2.cloned.1.call-done = bf16[256,8192]{1,0:T(8,128)(2,1)} async-done(((bf16[256,256]{1,0:T(8,128)(2,1)}), bf16[256,8192]{1,0:T(8,128)(2,1)}) %all-gather.2.cloned.1.call-update) | async-done | bytes 4194320 | tf_op jit(solution)/shard_map/while/body/eval_jaxpr/all_gather | solution.py:53
  476.4 123.8 %psum.37 = bf16[2,128,64]{1,2,0:T(8,128)(2,1)S(1)} all-reduce(bf16[2,128,64]{1,2,0:T(8,128)(2,1)S(1)} %pad_maximum_fusion.2), channel_id=1, replica_groups=mesh['section'=4,'mp'=32] {'mp'}, use_global_device_ids=true, to_apply=%region_7.7 | all-reduce | flops 16384 | bytes 65536 | tf_op jit(solution)/shard_map/while/body/eval_jaxpr/psum | solution.py:77
  613.8 62.7 %psum.36 = f32[256]{0:T(256)S(1)} all-reduce(f32[256]{0:T(256)S(1)} %get-tuple-element.499), channel_id=1, replica_groups=mesh['section'=4,'mp'=32] {'mp'}, use_global_device_ids=true, to_apply=%region_2.2 | all-reduce | flops 256 | bytes 2048 | tf_op jit(solution)/shard_map/while/body/eval_jaxpr/psum | solution.py:49
  680.3 42.9 %all-gather.2.cloned.1.call-done = bf16[256,8192]{1,0:T(8,128)(2,1)} async-done(((bf16[256,256]{1,0:T(8,128)(2,1)}), bf16[256,8192]{1,0:T(8,128)(2,1)}) %all-gather.2.cloned.1.call-update) | async-done | bytes 4194320 | tf_op jit(solution)/shard_map/while/body/eval_jaxpr/all_gather | solution.py:53
  723.2 129.1 %psum.37 = bf16[2,128,64]{1,2,0:T(8,128)(2,1)S(1)} all-reduce(bf16[2,128,64]{1,2,0:T(8,128)(2,1)S(1)} %pad_maximum_fusion.2), channel_id=1, replica_groups=mesh['section'=4,'mp'=32] {'mp'}, use_global_device_ids=true, to_apply=%region_7.7 | all-reduce | flops 16384 | bytes 65536 | tf_op jit(solution)/shard_map/while/body/eval_jaxpr/psum | solution.py:77
  863.7 62.7 %psum.36 = f32[256]{0:T(256)S(1)} all-reduce(f32[256]{0:T(256)S(1)} %get-tuple-element.499), channel_id=1, replica_groups=mesh['section'=4,'mp'=32] {'mp'}, use_global_device_ids=true, to_apply=%region_2.2 | all-reduce | flops 256 | bytes 2048 | tf_op jit(solution)/shard_map/while/body/eval_jaxpr/psum | solution.py:49
  930.2 42.4 %all-gather.2.cloned.1.call-done = bf16[256,8192]{1,0:T(8,128)(2,1)} async-done(((bf16[256,256]{1,0:T(8,128)(2,1)}), bf16[256,8192]{1,0:T(8,128)(2,1)}) %all-gather.2.cloned.1.call-update) | async-done | bytes 4194320 | tf_op jit(solution)/shard_map/while/body/eval_jaxpr/all_gather | solution.py:53
  972.6 126.5 %psum.37 = bf16[2,128,64]{1,2,0:T(8,128)(2,1)S(1)} all-reduce(bf16[2,128,64]{1,2,0:T(8,128)(2,1)S(1)} %pad_maximum_fusion.2), channel_id=1, replica_groups=mesh['section'=4,'mp'=32] {'mp'}, use_global_device_ids=true, to_apply=%region_7.7 | all-reduce | flops 16384 | bytes 65536 | tf_op jit(solution)/shard_map/while/body/eval_jaxpr/psum | solution.py:77
  1115.3 62.7 %psum.36 = f32[256]{0:T(256)S(1)} all-reduce(f32[256]{0:T(256)S(1)} %get-tuple-element.499), channel_id=1, replica_groups=mesh['section'=4,'mp'=32] {'mp'}, use_global_device_ids=true, to_apply=%region_2.2 | all-reduce | flops 256 | bytes 2048 | tf_op jit(solution)/shard_map/while/body/eval_jaxpr/psum | solution.py:49
  1181.8 41.3 %all-gather.2.cloned.1.call-done = bf16[256,8192]{1,0:T(8,128)(2,1)} async-done(((bf16[256,256]{1,0:T(8,128)(2,1)}), bf16[256,8192]{1,0:T(8,128)(2,1)}) %all-gather.2.cloned.1.call-update) | async-done | bytes 4194320 | tf_op jit(solution)/shard_map/while/body/eval_jaxpr/all_gather | solution.py:53
  1223.1 126.5 %psum.37 = bf16[2,128,64]{1,2,0:T(8,128)(2,1)S(1)} all-reduce(bf16[2,128,64]{1,2,0:T(8,128)(2,1)S(1)} %pad_maximum_fusion.2), channel_id=1, replica_groups=mesh['section'=4,'mp'=32] {'mp'}, use_global_device_ids=true, to_apply=%region_7.7 | all-reduce | flops 16384 | bytes 65536 | tf_op jit(solution)/shard_map/while/body/eval_jaxpr/psum | solution.py:77
  1363.1 62.7 %psum.36 = f32[256]{0:T(256)S(1)} all-reduce(f32[256]{0:T(256)S(1)} %get-tuple-element.499), channel_id=1, replica_groups=mesh['section'=4,'mp'=32] {'mp'}, use_global_device_ids=true, to_apply=%region_2.2 | all-reduce | flops 256 | bytes 2048 | tf_op jit(solution)/shard_map/while/body/eval_jaxpr/psum | solution.py:49
  1429.6 45.5 %all-gather.2.cloned.1.call-done = bf16[256,8192]{1,0:T(8,128)(2,1)} async-done(((bf16[256,256]{1,0:T(8,128)(2,1)}), bf16[256,8192]{1,0:T(8,128)(2,1)}) %all-gather.2.cloned.1.call-update) | async-done | bytes 4194320 | tf_op jit(solution)/shard_map/while/body/eval_jaxpr/all_gather | solution.py:53
  1475.2 126.5 %psum.37 = bf16[2,128,64]{1,2,0:T(8,128)(2,1)S(1)} all-reduce(bf16[2,128,64]{1,2,0:T(8,128)(2,1)S(1)} %pad_maximum_fusion.2), channel_id=1, replica_groups=mesh['section'=4,'mp'=32] {'mp'}, use_global_device_ids=true, to_apply=%region_7.7 | all-reduce | flops 16384 | bytes 65536 | tf_op jit(solution)/shard_map/while/body/eval_jaxpr/psum | solution.py:77
  1615.2 62.7 %psum.36 = f32[256]{0:T(256)S(1)} all-reduce(f32[256]{0:T(256)S(1)} %get-tuple-element.499), channel_id=1, replica_groups=mesh['section'=4,'mp'=32] {'mp'}, use_global_device_ids=true, to_apply=%region_2.2 | all-reduce | flops 256 | bytes 2048 | tf_op jit(solution)/shard_map/while/body/eval_jaxpr/psum | solution.py:49
  1681.7 45.3 %all-gather.2.cloned.1.call-done = bf16[256,8192]{1,0:T(8,128)(2,1)} async-done(((bf16[256,256]{1,0:T(8,128)(2,1)}), bf16[256,8192]{1,0:T(8,128)(2,1)}) %all-gather.2.cloned.1.call-update) | async-done | bytes 4194320 | tf_op jit(solution)/shard_map/while/body/eval_jaxpr/all_gather | solution.py:53
  1727.0 126.5 %psum.37 = bf16[2,128,64]{1,2,0:T(8,128)(2,1)S(1)} all-reduce(bf16[2,128,64]{1,2,0:T(8,128)(2,1)S(1)} %pad_maximum_fusion.2), channel_id=1, replica_groups=mesh['section'=4,'mp'=32] {'mp'}, use_global_device_ids=true, to_apply=%region_7.7 | all-reduce | flops 16384 | bytes 65536 | tf_op jit(solution)/shard_map/while/body/eval_jaxpr/psum | solution.py:77
  1881.8 64.6 %psum.31 = f32[1,256]{1,0:T(1,128)S(1)} all-reduce(f32[1,256]{1,0:T(1,128)S(1)} %bitcast.87), channel_id=1, replica_groups=mesh['section'=4,'mp'=32] {'mp'}, use_global_device_ids=true, to_apply=%region_11.12 | all-reduce | flops 256 | bytes 2048 | tf_op jit(solution)/shard_map/psum | solution.py:120
  (165 shorter events, 195.2 us)
Async XLA Ops:
  62.9 11.8 copy-start.1
  62.9 11.9 copy-start.2
  62.9 11.9 copy-start
  65.2 24.6 %all-to-all-start = ((bf16[32,2,8192]{2,1,0:T(2,128)(2,1)}), bf16[32,2,8192]{2,1,0:T(2,128)(2,1)S(1)}, u32[]{:S(2)}, u32[]{:S(2)}) async-start(bf16[32,2,8192]{2,1,0:T(2,128)(2,1)} %reshape.80), calls=%async_computation | async-start | bytes 2097152 | tf_op jit(solution)/shard_map/all_to_all | solution.py:39
  106.2 1753.5 %copy-start.3 = (bf16[256]{0:T(256)(128)(2,1)S(1)}, bf16[256]{0:T(256)(128)(2,1)}, u32[]{:S(2)}) copy-start(bf16[256]{0:T(256)(128)(2,1)} %param.19) | copy-start | bytes 1540
  106.2 1840.2 %copy-start.4 = (s32[1,2]{1,0:T(1,128)S(1)}, s32[1,2]{1,0:T(1,128)}, u32[]{:S(2)}) copy-start(s32[1,2]{1,0:T(1,128)} %param.21) | copy-start | bytes 28
  106.2 118.1 %all-gather.2.cloned.1.call-start = ((), (), s32[]{:S(2)}) async-start(), calls=%async_computation.3 | async-start | bytes 4325376 | tf_op jit(solution)/shard_map/while/body/eval_jaxpr/all_gather | solution.py:53
  106.2 6.8 collective-permute-start
  356.4 117.3 %all-gather.2.cloned.1.call-start = ((), (), s32[]{:S(2)}) async-start(), calls=%async_computation.3 | async-start | bytes 4325376 | tf_op jit(solution)/shard_map/while/body/eval_jaxpr/all_gather | solution.py:53
  357.4 6.0 collective-permute-start
  605.9 117.3 %all-gather.2.cloned.1.call-start = ((), (), s32[]{:S(2)}) async-start(), calls=%async_computation.3 | async-start | bytes 4325376 | tf_op jit(solution)/shard_map/while/body/eval_jaxpr/all_gather | solution.py:53
  606.8 6.0 collective-permute-start
  857.9 114.7 %all-gather.2.cloned.1.call-start = ((), (), s32[]{:S(2)}) async-start(), calls=%async_computation.3 | async-start | bytes 4325376 | tf_op jit(solution)/shard_map/while/body/eval_jaxpr/all_gather | solution.py:53
  858.8 3.8 collective-permute-start
  1104.7 118.4 %all-gather.2.cloned.1.call-start = ((), (), s32[]{:S(2)}) async-start(), calls=%async_computation.3 | async-start | bytes 4325376 | tf_op jit(solution)/shard_map/while/body/eval_jaxpr/all_gather | solution.py:53
  1105.7 8.6 collective-permute-start
  1355.2 119.9 %all-gather.2.cloned.1.call-start = ((), (), s32[]{:S(2)}) async-start(), calls=%async_computation.3 | async-start | bytes 4325376 | tf_op jit(solution)/shard_map/while/body/eval_jaxpr/all_gather | solution.py:53
  1356.1 6.0 collective-permute-start
  1607.3 119.7 %all-gather.2.cloned.1.call-start = ((), (), s32[]{:S(2)}) async-start(), calls=%async_computation.3 | async-start | bytes 4325376 | tf_op jit(solution)/shard_map/while/body/eval_jaxpr/all_gather | solution.py:53
  1608.2 6.0 collective-permute-start
  1859.1 21.6 %reduce-scatter.2.cloned.1.call-start = ((), (), s32[]{:S(2)}) async-start(), calls=%async_computation.2 | async-start | bytes 655360 | tf_op jit(solution)/shard_map/reduce_scatter | solution.py:111
Sparse Core Ops, SparseCore 0:
  178.3 45.9 all-gather.1
  428.0 45.7 all-gather.1
  677.4 45.7 all-gather.1
  927.3 45.2 all-gather.1
  1178.9 44.1 all-gather.1
  1426.7 48.3 all-gather.1
  1678.8 48.1 all-gather.1
Sparse Core Ops, SparseCore 1:
  1862.5 18.2 reduce-scatter.1
where the time goes:
time: 1960 us; the launch traced here: 1950 us
  blocking collectives  1400 us (71%)
  waiting for transfers between devices  343 us (18%)
  other arithmetic  65.1 us (3%)
  matrix products  44.3 us (2%)
  local copies, waits for them, and re-layouts  41.1 us (2%)
  starting transfers between devices  32.5 us (2%)
    psum x7, blocking collectives, layer_of_section(): lax.psum(compressed_projection.astype(jnp.bfloat16), 'mp')  885 us
    psum x7, blocking collectives, layer_of_section(): squares = lax.psum(jnp.sum(hidden_f * hidden_f, axis=1), 'mp')  439 us
    all_gather x7, waiting for transfers between devices, layer_of_section(): gathered = lax.all_gather(rescaled_activation, 'mp', axis=1, tiled=True)  303 us
    psum x1, blocking collectives, shards(): raw = lax.psum(partial_score, 'mp')  64.6 us
    unnamed x2, other arithmetic  45.2 us
  transfers between devices with their start and end apart: 16, of which 16 were waited for; matrix products, arithmetic and copies ran while one was open for 1% of the time, Pallas kernels for 0%

commit v1 on v0

--- a/solution.py
+++ b/solution.py
@@ -74,7 +74,9 @@
                 )
             )
         compressed_projection = jnp.stack(products)
-        compressed_projection = lax.psum(compressed_projection.astype(jnp.bfloat16), "mp")
+        compressed_projection = jnp.sum(
+            lax.all_gather(compressed_projection.astype(jnp.bfloat16), "mp"), axis=0
+        )
         chosen_expansion_matrix = (
             jnp.dot(onehot, up_table, preferred_element_type=jnp.float32)
             .astype(jnp.bfloat16)

time: 1960 us -> 1400 us (0.71)
  blocking collectives: 1400 us -> 529 us
  waiting for transfers between devices: 343 us -> 643 us
    psum x7 -> x0, blocking collectives: 885 us -> none  [layer_of_section(): lax.psum(compressed_projection.astype(jnp.bfloat16), 'mp')]
    all_gather x0 -> x7, waiting for transfers between devices: none -> 290 us  [layer_of_section(): lax.all_gather(compressed_projection.astype(jnp.bfloat16), 'mp')]
  transfers between devices with their start and end apart: 16 -> 23, of which waited for: 16 -> 23; matrix products, arithmetic and copies ran while one was open for 1% -> 1% of each run, Pallas kernels for 0% -> 0%
where the time goes in v1:
time: 1400 us; the launch traced here: 1390 us
  waiting for transfers between devices  643 us (46%)
  blocking collectives  529 us (38%)
  other arithmetic  73.7 us (5%)
  local copies, waits for them, and re-layouts  46.2 us (3%)
  matrix products  44.1 us (3%)
  starting transfers between devices  32.4 us (2%)
  between operations  15.3 us (1%)
    psum x7, blocking collectives, layer_of_section(): squares = lax.psum(jnp.sum(hidden_f * hidden_f, axis=1), 'mp')  449 us
    all_gather x7, waiting for transfers between devices, layer_of_section(): gathered = lax.all_gather(rescaled_activation, 'mp', axis=1, tiled=True)  307 us
    all_gather x7, waiting for transfers between devices, layer_of_section(): lax.all_gather(compressed_projection.astype(jnp.bfloat16), 'mp')  290 us
    psum x1, blocking collectives, shards(): raw = lax.psum(partial_score, 'mp')  64.6 us
    unnamed x2, other arithmetic  45.2 us
    dot_general x7, matrix products, layer_of_section(): base = jnp.dot(gathered, weight, preferred_element_type=jnp.float32)  37.7 us
  transfers between devices with their start and end apart: 23, of which 23 were waited for; matrix products, arithmetic and copies ran while one was open for 1% of the time, Pallas kernels for 0%

profile of v1, /device:TPU:0, one launch (start us, length us, event | category | flops | bytes accessed | tf_op | source)
XLA Modules:
  0.0 1394.1 jit_solution(7109522286773128321)
XLA Ops:
  17.7 45.2 %reduce.7 = bf16[8192,64]{1,0:T(8,128)(2,1)S(1)} reduce(bf16[8192,1,1,64]{3,2,1,0:T(2,128)(2,1)} %bitcast.80, bf16[]{:T(256)} %broadcast.115), dimensions={1,2}, to_apply=%bitcast.49.reduce_sub_computation | reduce | bytes 2097154
  106.2 1189.9 %while.18 = (s32[]{:T(128)}, bf16[256,256]{1,0:T(8,128)(2,1)S(1)}, bf16[4,256,256]{2,1,0:T(8,128)(2,1)}, pred[]{:T(512)}, bf16[4,256,256]{2,1,0:T(8,128)(2,1)}, ...) while((s32[]{:T(128)}, bf16[256,256]{1,0:T(8,128)(2,1)S(1)}, ...), condition=%wide.region_8.9_spmd.clone, body=%wide.region_0.8_spmd.clone.sunk | while | flops 1354203648 | bytes 36052464 | solution.py:112
  114.1 63.3 %psum.24 = f32[256]{0:T(256)S(1)} all-reduce(f32[256]{0:T(256)S(1)} %get-tuple-element.542), channel_id=1, replica_groups=mesh['section'=4,'mp'=32] {'mp'}, use_global_device_ids=true, to_apply=%region_2.2 | all-reduce | flops 256 | bytes 2048 | tf_op jit(solution)/shard_map/while/body/eval_jaxpr/psum | solution.py:49
  180.3 44.0 %all-gather.3.cloned.1.call-done = bf16[256,8192]{1,0:T(8,128)(2,1)} async-done(((bf16[256,256]{1,0:T(8,128)(2,1)}), bf16[256,8192]{1,0:T(8,128)(2,1)}) %all-gather.3.cloned.1.call-update) | async-done | bytes 4194320 | tf_op jit(solution)/shard_map/while/body/eval_jaxpr/all_gather | solution.py:53
  226.9 41.9 %all-gather.5.cloned.1.call-done = bf16[32,2,128,64]{2,3,1,0:T(8,128)(2,1)} async-done(((bf16[1,2,128,64]{2,3,1,0:T(8,128)(2,1)}), bf16[32,2,128,64]{2,3,1,0:T(8,128)(2,1)}) %all-gather.5.cloned.1.call-update) | async-done | bytes 1048592 | tf_op jit(solution)/shard_map/while/body/eval_jaxpr/all_gather | solution.py:78
  283.4 64.3 %psum.24 = f32[256]{0:T(256)S(1)} all-reduce(f32[256]{0:T(256)S(1)} %get-tuple-element.542), channel_id=1, replica_groups=mesh['section'=4,'mp'=32] {'mp'}, use_global_device_ids=true, to_apply=%region_2.2 | all-reduce | flops 256 | bytes 2048 | tf_op jit(solution)/shard_map/while/body/eval_jaxpr/psum | solution.py:49
  350.7 43.8 %all-gather.3.cloned.1.call-done = bf16[256,8192]{1,0:T(8,128)(2,1)} async-done(((bf16[256,256]{1,0:T(8,128)(2,1)}), bf16[256,8192]{1,0:T(8,128)(2,1)}) %all-gather.3.cloned.1.call-update) | async-done | bytes 4194320 | tf_op jit(solution)/shard_map/while/body/eval_jaxpr/all_gather | solution.py:53
  399.7 39.3 %all-gather.5.cloned.1.call-done = bf16[32,2,128,64]{2,3,1,0:T(8,128)(2,1)} async-done(((bf16[1,2,128,64]{2,3,1,0:T(8,128)(2,1)}), bf16[32,2,128,64]{2,3,1,0:T(8,128)(2,1)}) %all-gather.5.cloned.1.call-update) | async-done | bytes 1048592 | tf_op jit(solution)/shard_map/while/body/eval_jaxpr/all_gather | solution.py:78
  453.6 64.3 %psum.24 = f32[256]{0:T(256)S(1)} all-reduce(f32[256]{0:T(256)S(1)} %get-tuple-element.542), channel_id=1, replica_groups=mesh['section'=4,'mp'=32] {'mp'}, use_global_device_ids=true, to_apply=%region_2.2 | all-reduce | flops 256 | bytes 2048 | tf_op jit(solution)/shard_map/while/body/eval_jaxpr/psum | solution.py:49
  520.8 43.8 %all-gather.3.cloned.1.call-done = bf16[256,8192]{1,0:T(8,128)(2,1)} async-done(((bf16[256,256]{1,0:T(8,128)(2,1)}), bf16[256,8192]{1,0:T(8,128)(2,1)}) %all-gather.3.cloned.1.call-update) | async-done | bytes 4194320 | tf_op jit(solution)/shard_map/while/body/eval_jaxpr/all_gather | solution.py:53
  567.2 41.9 %all-gather.5.cloned.1.call-done = bf16[32,2,128,64]{2,3,1,0:T(8,128)(2,1)} async-done(((bf16[1,2,128,64]{2,3,1,0:T(8,128)(2,1)}), bf16[32,2,128,64]{2,3,1,0:T(8,128)(2,1)}) %all-gather.5.cloned.1.call-update) | async-done | bytes 1048592 | tf_op jit(solution)/shard_map/while/body/eval_jaxpr/all_gather | solution.py:78
  623.8 64.3 %psum.24 = f32[256]{0:T(256)S(1)} all-reduce(f32[256]{0:T(256)S(1)} %get-tuple-element.542), channel_id=1, replica_groups=mesh['section'=4,'mp'=32] {'mp'}, use_global_device_ids=true, to_apply=%region_2.2 | all-reduce | flops 256 | bytes 2048 | tf_op jit(solution)/shard_map/while/body/eval_jaxpr/psum | solution.py:49
  691.0 43.8 %all-gather.3.cloned.1.call-done = bf16[256,8192]{1,0:T(8,128)(2,1)} async-done(((bf16[256,256]{1,0:T(8,128)(2,1)}), bf16[256,8192]{1,0:T(8,128)(2,1)}) %all-gather.3.cloned.1.call-update) | async-done | bytes 4194320 | tf_op jit(solution)/shard_map/while/body/eval_jaxpr/all_gather | solution.py:53
  737.4 41.9 %all-gather.5.cloned.1.call-done = bf16[32,2,128,64]{2,3,1,0:T(8,128)(2,1)} async-done(((bf16[1,2,128,64]{2,3,1,0:T(8,128)(2,1)}), bf16[32,2,128,64]{2,3,1,0:T(8,128)(2,1)}) %all-gather.5.cloned.1.call-update) | async-done | bytes 1048592 | tf_op jit(solution)/shard_map/while/body/eval_jaxpr/all_gather | solution.py:78
  794.0 64.3 %psum.24 = f32[256]{0:T(256)S(1)} all-reduce(f32[256]{0:T(256)S(1)} %get-tuple-element.542), channel_id=1, replica_groups=mesh['section'=4,'mp'=32] {'mp'}, use_global_device_ids=true, to_apply=%region_2.2 | all-reduce | flops 256 | bytes 2048 | tf_op jit(solution)/shard_map/while/body/eval_jaxpr/psum | solution.py:49
  861.2 43.8 %all-gather.3.cloned.1.call-done = bf16[256,8192]{1,0:T(8,128)(2,1)} async-done(((bf16[256,256]{1,0:T(8,128)(2,1)}), bf16[256,8192]{1,0:T(8,128)(2,1)}) %all-gather.3.cloned.1.call-update) | async-done | bytes 4194320 | tf_op jit(solution)/shard_map/while/body/eval_jaxpr/all_gather | solution.py:53
  907.5 41.8 %all-gather.5.cloned.1.call-done = bf16[32,2,128,64]{2,3,1,0:T(8,128)(2,1)} async-done(((bf16[1,2,128,64]{2,3,1,0:T(8,128)(2,1)}), bf16[32,2,128,64]{2,3,1,0:T(8,128)(2,1)}) %all-gather.5.cloned.1.call-update) | async-done | bytes 1048592 | tf_op jit(solution)/shard_map/while/body/eval_jaxpr/all_gather | solution.py:78
  964.0 64.3 %psum.24 = f32[256]{0:T(256)S(1)} all-reduce(f32[256]{0:T(256)S(1)} %get-tuple-element.542), channel_id=1, replica_groups=mesh['section'=4,'mp'=32] {'mp'}, use_global_device_ids=true, to_apply=%region_2.2 | all-reduce | flops 256 | bytes 2048 | tf_op jit(solution)/shard_map/while/body/eval_jaxpr/psum | solution.py:49
  1031.2 43.8 %all-gather.3.cloned.1.call-done = bf16[256,8192]{1,0:T(8,128)(2,1)} async-done(((bf16[256,256]{1,0:T(8,128)(2,1)}), bf16[256,8192]{1,0:T(8,128)(2,1)}) %all-gather.3.cloned.1.call-update) | async-done | bytes 4194320 | tf_op jit(solution)/shard_map/while/body/eval_jaxpr/all_gather | solution.py:53
  1077.6 41.6 %all-gather.5.cloned.1.call-done = bf16[32,2,128,64]{2,3,1,0:T(8,128)(2,1)} async-done(((bf16[1,2,128,64]{2,3,1,0:T(8,128)(2,1)}), bf16[32,2,128,64]{2,3,1,0:T(8,128)(2,1)}) %all-gather.5.cloned.1.call-update) | async-done | bytes 1048592 | tf_op jit(solution)/shard_map/while/body/eval_jaxpr/all_gather | solution.py:78
  1133.9 64.3 %psum.24 = f32[256]{0:T(256)S(1)} all-reduce(f32[256]{0:T(256)S(1)} %get-tuple-element.542), channel_id=1, replica_groups=mesh['section'=4,'mp'=32] {'mp'}, use_global_device_ids=true, to_apply=%region_2.2 | all-reduce | flops 256 | bytes 2048 | tf_op jit(solution)/shard_map/while/body/eval_jaxpr/psum | solution.py:49
  1201.1 43.8 %all-gather.3.cloned.1.call-done = bf16[256,8192]{1,0:T(8,128)(2,1)} async-done(((bf16[256,256]{1,0:T(8,128)(2,1)}), bf16[256,8192]{1,0:T(8,128)(2,1)}) %all-gather.3.cloned.1.call-update) | async-done | bytes 4194320 | tf_op jit(solution)/shard_map/while/body/eval_jaxpr/all_gather | solution.py:53
  1247.5 41.5 %all-gather.5.cloned.1.call-done = bf16[32,2,128,64]{2,3,1,0:T(8,128)(2,1)} async-done(((bf16[1,2,128,64]{2,3,1,0:T(8,128)(2,1)}), bf16[32,2,128,64]{2,3,1,0:T(8,128)(2,1)}) %all-gather.5.cloned.1.call-update) | async-done | bytes 1048592 | tf_op jit(solution)/shard_map/while/body/eval_jaxpr/all_gather | solution.py:78
  1321.7 64.6 %psum.21 = f32[1,256]{1,0:T(1,128)S(1)} all-reduce(f32[1,256]{1,0:T(1,128)S(1)} %bitcast.87), channel_id=1, replica_groups=mesh['section'=4,'mp'=32] {'mp'}, use_global_device_ids=true, to_apply=%region_11.12 | all-reduce | flops 256 | bytes 2048 | tf_op jit(solution)/shard_map/psum | solution.py:122
  (186 shorter events, 215.4 us)
Async XLA Ops:
  65.2 24.6 %all-to-all-start = ((bf16[32,2,8192]{2,1,0:T(2,128)(2,1)}), bf16[32,2,8192]{2,1,0:T(2,128)(2,1)S(1)}, u32[]{:S(2)}, u32[]{:S(2)}) async-start(bf16[32,2,8192]{2,1,0:T(2,128)(2,1)} %reshape.119), calls=%async_computation | async-start | bytes 2097152 | tf_op jit(solution)/shard_map/all_to_all | solution.py:39
  106.2 1280.1 %copy-start.4 = (s32[1,2]{1,0:T(1,128)S(1)}, s32[1,2]{1,0:T(1,128)}, u32[]{:S(2)}) copy-start(s32[1,2]{1,0:T(1,128)} %param.21) | copy-start | bytes 28
  106.2 118.1 %all-gather.3.cloned.1.call-start = ((), (), s32[]{:S(2)}) async-start(), calls=%async_computation.3 | async-start | bytes 4325376 | tf_op jit(solution)/shard_map/while/body/eval_jaxpr/all_gather | solution.py:53
  106.2 6.8 collective-permute-start
  178.2 90.6 %all-gather.5.cloned.1.call-start = ((), (), s32[]{:S(2)}) async-start(), calls=%async_computation.4 | async-start | bytes 1081344 | tf_op jit(solution)/shard_map/while/body/eval_jaxpr/all_gather | solution.py:78
  275.8 118.7 %all-gather.3.cloned.1.call-start = ((), (), s32[]{:S(2)}) async-start(), calls=%async_computation.3 | async-start | bytes 4325376 | tf_op jit(solution)/shard_map/while/body/eval_jaxpr/all_gather | solution.py:53
  275.8 6.6 collective-permute-start
  348.5 90.4 %all-gather.5.cloned.1.call-start = ((), (), s32[]{:S(2)}) async-start(), calls=%async_computation.4 | async-start | bytes 1081344 | tf_op jit(solution)/shard_map/while/body/eval_jaxpr/all_gather | solution.py:78
  446.0 118.7 %all-gather.3.cloned.1.call-start = ((), (), s32[]{:S(2)}) async-start(), calls=%async_computation.3 | async-start | bytes 4325376 | tf_op jit(solution)/shard_map/while/body/eval_jaxpr/all_gather | solution.py:53
  446.0 6.6 collective-permute-start
  518.7 90.4 %all-gather.5.cloned.1.call-start = ((), (), s32[]{:S(2)}) async-start(), calls=%async_computation.4 | async-start | bytes 1081344 | tf_op jit(solution)/shard_map/while/body/eval_jaxpr/all_gather | solution.py:78
  616.2 118.7 %all-gather.3.cloned.1.call-start = ((), (), s32[]{:S(2)}) async-start(), calls=%async_computation.3 | async-start | bytes 4325376 | tf_op jit(solution)/shard_map/while/body/eval_jaxpr/all_gather | solution.py:53
  616.2 6.6 collective-permute-start
  688.9 90.4 %all-gather.5.cloned.1.call-start = ((), (), s32[]{:S(2)}) async-start(), calls=%async_computation.4 | async-start | bytes 1081344 | tf_op jit(solution)/shard_map/while/body/eval_jaxpr/all_gather | solution.py:78
  786.3 118.7 %all-gather.3.cloned.1.call-start = ((), (), s32[]{:S(2)}) async-start(), calls=%async_computation.3 | async-start | bytes 4325376 | tf_op jit(solution)/shard_map/while/body/eval_jaxpr/all_gather | solution.py:53
  786.3 6.6 collective-permute-start
  859.1 90.3 %all-gather.5.cloned.1.call-start = ((), (), s32[]{:S(2)}) async-start(), calls=%async_computation.4 | async-start | bytes 1081344 | tf_op jit(solution)/shard_map/while/body/eval_jaxpr/all_gather | solution.py:78
  956.4 118.7 %all-gather.3.cloned.1.call-start = ((), (), s32[]{:S(2)}) async-start(), calls=%async_computation.3 | async-start | bytes 4325376 | tf_op jit(solution)/shard_map/while/body/eval_jaxpr/all_gather | solution.py:53
  956.4 6.6 collective-permute-start
  1029.1 90.1 %all-gather.5.cloned.1.call-start = ((), (), s32[]{:S(2)}) async-start(), calls=%async_computation.4 | async-start | bytes 1081344 | tf_op jit(solution)/shard_map/while/body/eval_jaxpr/all_gather | solution.py:78
  1126.2 118.7 %all-gather.3.cloned.1.call-start = ((), (), s32[]{:S(2)}) async-start(), calls=%async_computation.3 | async-start | bytes 4325376 | tf_op jit(solution)/shard_map/while/body/eval_jaxpr/all_gather | solution.py:53
  1126.3 6.6 collective-permute-start
  1199.0 90.1 %all-gather.5.cloned.1.call-start = ((), (), s32[]{:S(2)}) async-start(), calls=%async_computation.4 | async-start | bytes 1081344 | tf_op jit(solution)/shard_map/while/body/eval_jaxpr/all_gather | solution.py:78
  1296.1 24.6 %reduce-scatter.2.cloned.1.call-start = ((), (), s32[]{:S(2)}) async-start(), calls=%async_computation.2 | async-start | bytes 655360 | tf_op jit(solution)/shard_map/reduce_scatter | solution.py:113
  (4 other events, 1226.0 us)
Sparse Core Ops, SparseCore 0:
  178.3 45.9 all-gather.2
  226.5 42.1 all-gather.4
  348.7 45.7 all-gather.2
  397.9 41.0 all-gather.4
  518.8 45.7 all-gather.2
  566.8 42.3 all-gather.4
  689.0 45.7 all-gather.2
  737.1 42.1 all-gather.4
  859.2 45.7 all-gather.2
  907.1 42.2 all-gather.4
  1029.2 45.7 all-gather.2
  1077.2 42.0 all-gather.4
  1199.1 45.7 all-gather.2
  1247.0 41.9 all-gather.4
Sparse Core Ops, SparseCore 1:
  1299.5 21.2 reduce-scatter.1
